TPU v7x, 32 devices: a whole 2x2x4 slice. The times are simulated.
32 devices in a mesh: prow: 8 (over z, core), pcol: 4 (over y, x).
Axes of the slice: x: 2, y: 2, z: 4, core: 2. Of those that a mesh axis runs over, the one named last changes fastest.
Arguments:
- right_side: float32 [1024, 4, 4, 1024], P('prow', None, 'pcol'), may hold values from -6 to 6
- inverse_blocks: bfloat16 [2, 1, 8, 1024, 2, 4, 1024], P(None, None, 'prow', None, None, 'pcol'), as said below
- coupling: bfloat16 [1, 8, 1024, 2, 4, 1024], P(None, 'prow', None, None, 'pcol'), may hold values from -0.03125 to 0.03125
- pivots: int32 [2, 8, 1024], P(None, 'prow'), may hold values from 0 to 16383, as said below
Outputs:
- solution: bfloat16 [1024, 2, 8, 1024], P('pcol', None, 'prow')
Inputs may be any that keep to these rules, and one draw needn't show every extreme that they name: `inverse_blocks`: each block is unit upper triangular: ones on its diagonal, zeros below it. Every row number of the window appears exactly once; for every p and p2, exactly 16 * 1024 / 8 ** 2 of the entries pivots[:, p, :] are rows g with (g // 1024) % 8 == p2.
All inputs are finite; a program needn't handle non-finite values.
Results may differ from a plain program's by a relative error of at most 0.0052.
Values may be sent and summed in bfloat16 or wider, within the bound.
A program may use at most 128 MiB of HBM per device.

v0:
```python
import jax
import jax.numpy as jnp
from jax import lax
from jax.sharding import PartitionSpec as P


def body(right_side, inverse_blocks, coupling, pivots):
    bf16 = jnp.bfloat16
    f32 = jnp.float32
    rhs_here = right_side.shape[0]
    tiles_across = right_side.shape[1]
    tile_width = right_side.shape[3]
    blocks_here = inverse_blocks.shape[1]
    count_rows = blocks_here * tile_width
    tiles_half = inverse_blocks.shape[4]
    count_cols = tiles_half * tile_width
    inverse_pair = inverse_blocks.reshape(2, count_rows, count_cols)
    coupling_mat = coupling.reshape(count_rows, count_cols)
    rows_axis = lax.axis_size("prow")
    cols_axis = lax.axis_size("pcol")
    own_cols = rhs_here * rows_axis // cols_axis
    contract_last = (((1,), (1,)), ((), ()))
    me = lax.axis_index("prow")
    lower_rhs = right_side[:, :tiles_half].reshape(rhs_here, count_cols)
    upper_rhs = right_side[:, tiles_half:].astype(bf16).reshape(rhs_here, count_cols)
    own_pivots = pivots.reshape(-1)
    width = own_pivots.shape[0]
    share = width // rows_axis
    all_pivots = lax.all_gather(own_pivots, "prow", axis=0)

    def owner_of(rows):
        return rows // tile_width % rows_axis

    def local_of(rows):
        return rows // (tile_width * rows_axis) * tile_width + rows % tile_width

    mine = owner_of(all_pivots) == me
    slot = jnp.where(mine, jnp.cumsum(mine.astype(jnp.int32), axis=1) - 1, -1)
    hits = slot[:, :, None] == lax.broadcasted_iota(jnp.int32, (1, 1, share), 2)
    picked = jnp.sum(jnp.where(hits, local_of(all_pivots)[:, :, None], 0), axis=1)
    owner = owner_of(own_pivots)
    same = owner[None, :] == lax.broadcasted_iota(jnp.int32, (rows_axis, 1), 0)
    rank = jnp.sum(jnp.where(same, jnp.cumsum(same.astype(jnp.int32), axis=1) - 1, 0), axis=0)
    code = owner * share + rank

    def solve_with(inverse_mat, portion):
        return lax.dot_general(portion, inverse_mat, contract_last, preferred_element_type=bf16)

    first_partial = solve_with(
        inverse_pair[1], lax.all_gather(upper_rhs, "prow", axis=0, tiled=True)
    )
    upper_solved = lax.psum_scatter(first_partial, "pcol", scatter_dimension=0, tiled=True)
    update_partial = jnp.dot(
        lax.all_gather(upper_solved, "pcol", axis=0, tiled=True),
        coupling_mat,
        preferred_element_type=bf16,
    )
    update = lax.psum_scatter(update_partial, "prow", scatter_dimension=0, tiled=True)
    lower_ready = (lower_rhs - update.astype(f32)).astype(bf16)
    second_partial = solve_with(
        inverse_pair[0], lax.all_gather(lower_ready, "prow", axis=0, tiled=True)
    )
    lower_solved = lax.psum_scatter(second_partial, "pcol", scatter_dimension=0, tiled=True)
    joined = jnp.concatenate([lower_solved, upper_solved], axis=1)
    choose = (picked.reshape(-1)[None, :] == lax.broadcasted_iota(jnp.int32, (width, 1), 0)).astype(
        bf16
    )
    chosen = jnp.dot(joined, choose, preferred_element_type=bf16)
    received = lax.all_to_all(
        chosen.reshape(own_cols, rows_axis, share), "prow", split_axis=1, concat_axis=1
    ).reshape(own_cols, width)
    place = (code[None, :] == lax.broadcasted_iota(jnp.int32, (width, 1), 0)).astype(bf16)
    permuted = jnp.dot(received, place, preferred_element_type=bf16)
    return permuted.reshape(own_cols, pivots.shape[0], 1, tile_width)


def solution(mesh):
    in_specs = (
        P("prow", None, "pcol", None),
        P(None, None, "prow", None, None, "pcol", None),
        P(None, "prow", None, None, "pcol", None),
        P(None, "prow", None),
    )
    out_specs = P("pcol", None, "prow", None)
    return jax.shard_map(body, mesh=mesh, in_specs=in_specs, out_specs=out_specs, check_vma=False)
```

profile of v0, /device:TPU:0, one launch (start us, length us, event | category | flops | bytes accessed | tf_op | source)
XLA Modules:
  0.0 343.2 jit_solution(7763216155621803395)
XLA Ops:
  6.5 4.5 %fusion.9 = bf16[128,2,1024]{2,1,0:T(2,128)(2,1)S(1)} fusion(f32[128,4,1,1024]{3,2,1,0:T(1,128)} %param.4), kind=kLoop, calls=%fused_computation.12 | loop fusion | bytes 1048576 | tf_op jit(solution)/shard_map/slice | solution.py:25
  11.0 0.9 copy.21
  12.0 0.0 all-gather.5.cloned.1.call-update
  12.0 0.0 reduce-scatter.4.cloned.1.call-start
  12.0 8.0 %fusion.32 = (bf16[1,1,1,1024,2,1,1024]{6,4,5,3,2,1,0:T(2,128)(2,1)}, bf16[1,1,1,1024,2,1,1024]{6,4,5,3,2,1,0:T(2,128)(2,1)S(1)}) fusion(bf16[2,1,1,1024,2,1,1024]{6,4,5,3,2,1,0:T(2,128)(2,1)} %param.5), kind=kLoop, calls=%fused_computation.72 | loop fusion | bytes 16777216 | tf_op jit(solution)/shard_map/slice | solution.py:61
  20.0 3.4 copy.22
  23.4 38.3 %all-gather.5.cloned.1.call-done = bf16[1024,2048]{1,0:T(8,128)(2,1)} async-done(((bf16[128,2048]{1,0:T(8,128)(2,1)}), bf16[1024,2048]{1,0:T(8,128)(2,1)}) %all-gather.5.cloned.1.call-update) | async-done | bytes 4194320 | tf_op jit(solution)/shard_map/all_gather | solution.py:50
  61.7 9.4 %fusion.33 = bf16[1024,1024]{1,0:T(8,128)(2,1)} fusion(bf16[1024,2048]{1,0:T(8,128)(2,1)} %all-gather.5.cloned.1.call-done, bf16[1024,2048]{1,0:T(8,128)(2,1)} %bitcast.86), kind=kOutput, calls=%fused_computation.73 | convolution fusion | flops 4294967296 | bytes 10485760 | tf_op jit(solution)/shard_map/dot_general | solution.py:47
  71.1 0.0 all-gather.7.cloned.1.call-start
  71.2 34.1 %reduce-scatter.4.cloned.1.call-done = bf16[256,1024]{1,0:T(8,128)(2,1)} async-done(((bf16[1024,1024]{1,0:T(8,128)(2,1)}), bf16[256,1024]{1,0:T(8,128)(2,1)}) %reduce-scatter.4.cloned.1.call-update) | async-done | bytes 524304 | tf_op jit(solution)/shard_map/reduce_scatter | solution.py:52
  105.3 0.0 all-gather.7.cloned.1.call-update
  105.3 0.2 reduce-scatter.6.cloned.1.call-start
  105.5 5.6 %copy.23 = bf16[128,8,2,1024]{3,1,2,0:T(8,128)(2,1)} copy(bf16[128,8,2,1024]{3,2,1,0:T(2,128)(2,1)} %bitcast.85) | data formatting | bytes 8388608
  111.1 31.2 %all-gather.7.cloned.1.call-done = bf16[1024,1024]{1,0:T(8,128)(2,1)} async-done(((bf16[256,1024]{1,0:T(8,128)(2,1)}), bf16[1024,1024]{1,0:T(8,128)(2,1)}) %all-gather.7.cloned.1.call-update) | async-done | bytes 2097168 | tf_op jit(solution)/shard_map/all_gather | solution.py:54
  142.3 9.3 %fusion.34 = bf16[1024,2048]{1,0:T(8,128)(2,1)} fusion(bf16[1024,1024]{1,0:T(8,128)(2,1)} %all-gather.7.cloned.1.call-done, bf16[1024,2048]{1,0:T(8,128)(2,1)} %bitcast.88), kind=kOutput, calls=%fused_computation.74 | convolution fusion | flops 4294967296 | bytes 10485760 | tf_op jit(solution)/shard_map/dot_general | solution.py:53
  151.6 0.0 reduce-scatter.6.cloned.1.call-update
  151.6 0.0 all-gather.9.cloned.1.call-start
  151.7 1.5 copy-done
  153.2 3.2 slice_reduce_fusion
  156.4 0.3 copy.20
  156.8 45.0 %reduce-scatter.6.cloned.1.call-done = bf16[128,2048]{1,0:T(8,128)(2,1)} async-done(((bf16[1024,2048]{1,0:T(8,128)(2,1)}), bf16[128,2048]{1,0:T(8,128)(2,1)}) %reduce-scatter.6.cloned.1.call-update) | async-done | bytes 524304 | tf_op jit(solution)/shard_map/reduce_scatter | solution.py:58
  201.7 1.9 subtract_convert_fusion
  203.7 0.3 reduce-scatter.8.cloned.1.call-start
  204.0 5.6 %copy.24 = bf16[128,8,2,1024]{3,1,2,0:T(8,128)(2,1)} copy(bf16[128,8,2,1024]{3,2,1,0:T(2,128)(2,1)} %bitcast.83) | data formatting | bytes 8388608
  209.6 39.6 %all-gather.9.cloned.1.call-done = bf16[1024,2048]{1,0:T(8,128)(2,1)} async-done(((bf16[128,2048]{1,0:T(8,128)(2,1)}), bf16[1024,2048]{1,0:T(8,128)(2,1)}) %all-gather.9.cloned.1.call-update) | async-done | bytes 4194320 | tf_op jit(solution)/shard_map/all_gather | solution.py:61
  249.2 9.4 %fusion.35 = bf16[1024,1024]{1,0:T(8,128)(2,1)} fusion(bf16[1024,2048]{1,0:T(8,128)(2,1)} %all-gather.9.cloned.1.call-done, bf16[1024,2048]{1,0:T(8,128)(2,1)} %bitcast.87), kind=kOutput, calls=%fused_computation.75 | convolution fusion | flops 4294967296 | bytes 10485760 | tf_op jit(solution)/shard_map/dot_general | solution.py:47
  258.6 0.0 reduce-scatter.8.cloned.1.call-update
  258.6 14.0 %all-gather = s32[8,1,2048]{2,1,0:T(1,128)S(1)} all-gather(s32[1,1,2048]{2,1,0:T(1,128)S(1)} %bitcast.94), channel_id=1, replica_groups=mesh['prow'=8,'pcol'=4] {'prow'}, dimensions={0}, use_global_device_ids=true | all-gather | bytes 73728 | tf_op jit(solution)/shard_map/all_gather | solution.py:29
  272.6 0.1 convert_bitcast_fusion
  272.7 2.3 reduce-window.14
  275.0 0.3 slice_reduce_fusion.2
  275.3 0.2 reduce-window.15
  275.4 0.1 add_bitcast_fusion
  275.5 0.1 fusion.17
  275.6 5.7 %select_reduce_fusion = s32[8,256]{1,0:T(8,128)S(1)} fusion(s32[8,2048]{1,0:T(8,128)S(1)} %get-tuple-element.9, s32[8,2048]{1,0:T(8,128)S(1)} %get-tuple-element.10), kind=kLoop, calls=%fused_computation.2 | loop fusion | flops 12580864 | bytes 139264 | tf_op jit(solution)/shard_map/reduce_sum | solution.py:40
  281.4 11.3 %reduce-scatter.8.cloned.1.call-done = bf16[256,1024]{1,0:T(8,128)(2,1)} async-done(((bf16[1024,1024]{1,0:T(8,128)(2,1)}), bf16[256,1024]{1,0:T(8,128)(2,1)}) %reduce-scatter.8.cloned.1.call-update) | async-done | bytes 524304 | tf_op jit(solution)/shard_map/reduce_scatter | solution.py:63
  292.7 4.4 %fusion.3 = bf16[256,2048]{1,0:T(8,128)(2,1)S(1)} fusion(s32[2048]{0:T(1024)S(1)} %bitcast.99, bf16[256,1024]{1,0:T(8,128)(2,1)S(1)} %copy-done.1, bf16[256,1024]{1,0:T(8,128)(2,1)} %reduce-scatter.8.cloned.1.call-done), kind=kOutput, calls=%fused_computation.6 | convolution fusion | flops 2153775104 | bytes 2105344 | tf_op jit(solution)/shard_map/dot_general | solution.py:68
  297.1 1.0 copy.38
  298.2 4.6 %all-to-all-start = ((bf16[256,8,256]{2,0,1:T(8,128)(2,1)}), bf16[256,8,256]{2,0,1:T(8,128)(2,1)S(1)}, u32[]{:S(2)}, u32[]{:S(2)}) async-start(bf16[256,8,256]{2,0,1:T(8,128)(2,1)} %bitcast.80), calls=%async_computation.3 | async-start | bytes 2097152 | tf_op jit(solution)/shard_map/all_to_all | solution.py:69
  302.8 2.3 reduce-window.16
  305.1 0.3 slice_reduce_fusion.1
  305.4 0.2 reduce-window.19
  305.6 0.1 select_reduce_fusion.1
  305.7 23.6 %all-to-all-done = bf16[256,8,256]{2,0,1:T(8,128)(2,1)S(1)} async-done(((bf16[256,8,256]{2,0,1:T(8,128)(2,1)}), bf16[256,8,256]{2,0,1:T(8,128)(2,1)S(1)}, u32[]{:S(2)}, u32[]{:S(2)}) %all-to-all-start) | async-done | bytes 1048608 | tf_op jit(solution)/shard_map/all_to_all | solution.py:69
  329.4 0.6 copy.15
  330.0 0.5 reshape.153
  330.5 3.8 %fusion.6 = bf16[256,2,1,1024]{3,0,1,2:T(8,128)(2,1)S(1)} fusion(bf16[256,2048,1]{1,0,2:T(8,128)(2,1)S(1)} %reshape.153, s32[2,1024]{1,0:T(2,128)S(1)} %fusion.27), kind=kOutput, calls=%fused_computation.9 | convolution fusion | flops 2151677952 | bytes 2105344 | tf_op jit(solution)/shard_map/dot_general | solution.py:73
  334.3 2.0 copy.16
  (14 shorter events, 0.1 us)
Async XLA Ops:
  6.5 55.2 %all-gather.5.cloned.1.call-start = ((), (), s32[]{:S(2)}) async-start(), calls=%async_computation.4 | async-start | bytes 4718592 | tf_op jit(solution)/shard_map/all_gather | solution.py:50
  12.0 93.3 %reduce-scatter.4.cloned.1.call-start = ((), (), s32[]{:S(2)}) async-start(), calls=%async_computation.5 | async-start | bytes 2621440 | tf_op jit(solution)/shard_map/reduce_scatter | solution.py:52
  71.1 71.2 %all-gather.7.cloned.1.call-start = ((), (), s32[]{:S(2)}) async-start(), calls=%async_computation.6 | async-start | bytes 2621440 | tf_op jit(solution)/shard_map/all_gather | solution.py:54
  105.3 96.4 %reduce-scatter.6.cloned.1.call-start = ((), (), s32[]{:S(2)}) async-start(), calls=%async_computation.7 | async-start | bytes 4718592 | tf_op jit(solution)/shard_map/reduce_scatter | solution.py:58
  151.6 1.6 copy-start
  151.6 97.5 %all-gather.9.cloned.1.call-start = ((), (), s32[]{:S(2)}) async-start(), calls=%async_computation.8 | async-start | bytes 4718592 | tf_op jit(solution)/shard_map/all_gather | solution.py:61
  203.7 89.0 %reduce-scatter.8.cloned.1.call-start = ((), (), s32[]{:S(2)}) async-start(), calls=%async_computation.9 | async-start | bytes 2621440 | tf_op jit(solution)/shard_map/reduce_scatter | solution.py:63
  249.2 9.4 %copy-start.2 = (s32[2,1,1024]{2,1,0:T(1,128)S(1)}, s32[2,1,1024]{2,1,0:T(1,128)}, u32[]{:S(2)}) copy-start(s32[2,1,1024]{2,1,0:T(1,128)} %param.7) | copy-start | bytes 24580
  249.2 43.5 %copy-start.1 = (bf16[256,1024]{1,0:T(8,128)(2,1)S(1)}, bf16[256,1024]{1,0:T(8,128)(2,1)}, u32[]{:S(2)}) copy-start(bf16[256,1024]{1,0:T(8,128)(2,1)} %reduce-scatter.4.cloned.1.call-done) | copy-start | bytes 1572868
  298.2 31.2 %all-to-all-start = ((bf16[256,8,256]{2,0,1:T(8,128)(2,1)}), bf16[256,8,256]{2,0,1:T(8,128)(2,1)S(1)}, u32[]{:S(2)}, u32[]{:S(2)}) async-start(bf16[256,8,256]{2,0,1:T(8,128)(2,1)} %bitcast.80), calls=%async_computation.3 | async-start | bytes 2097152 | tf_op jit(solution)/shard_map/all_to_all | solution.py:69
Sparse Core Ops, SparseCore 0:
  12.1 49.5 all-gather.4
  71.2 33.9 reduce-scatter.3
  107.1 35.1 all-gather.6
  151.8 49.9 reduce-scatter.5
  203.8 45.3 all-gather.8
  258.7 33.9 reduce-scatter.7
where the time goes:
time: 344 us; the launch traced here: 343 us
  waiting for transfers between devices  223 us (65%)
  local copies, waits for them, and re-layouts  37.9 us (11%)
  matrix products  36.2 us (11%)
  blocking collectives  14 us (4%)
  between operations  13.6 us (4%)
  other arithmetic  13 us (4%)
  starting transfers between devices  5.24 us (2%)
    reduce_scatter x1, waiting for transfers between devices, body(): lax.psum_scatter(update_partial, 'prow', scatter_dimension=0, tiled=True)  45 us
    all_gather x1, waiting for transfers between devices, body(): lax.all_gather(lower_ready, 'prow', axis=0, tiled=True)  39.6 us
    all_gather x1, waiting for transfers between devices, body(): lax.all_gather(upper_rhs, 'prow', axis=0, tiled=True)  38.3 us
    reduce_scatter x1, waiting for transfers between devices, body(): lax.psum_scatter(first_partial, 'pcol', scatter_dimension=0, tiled=True)  34.1 us
    all_gather x1, waiting for transfers between devices, body(): lax.all_gather(upper_solved, 'pcol', axis=0, tiled=True)  31.2 us
    all_to_all x1, waiting for transfers between devices, body(): lax.all_to_all(chosen.reshape(own_cols, rows_axis, share), 'prow', split_...  23.6 us
    dot_general x2, matrix products, solve_with(): lax.dot_general(portion, inverse_mat, contract_last, preferred_element_ty...  18.7 us
    unnamed x12, local copies, waits for them, and re-layouts  17.4 us
  transfers between devices with their start and end apart: 7, of which 7 were waited for; matrix products, arithmetic and copies ran while one was open for 11% of the time, Pallas kernels for 0%

commit v1 on v0

--- a/solution.py
+++ b/solution.py
@@ -2,6 +2,27 @@
 import jax.numpy as jnp
 from jax import lax
 from jax.sharding import PartitionSpec as P
+
+
+def in_order(blocks, dim):
+    shape = list(blocks.shape[1:])
+    shape[dim] *= blocks.shape[0]
+    return jnp.moveaxis(blocks, 0, dim).reshape(shape)
+
+
+def doubled(x, axis):
+    devices, position = (lax.axis_size(axis), lax.axis_index(axis))
+    blocks, bit = (x[None], 1)
+    while bit < devices:
+        theirs = lax.ppermute(blocks, axis, [(i, i ^ bit) for i in range(devices)])
+        low = position & bit == 0
+        blocks = jnp.concatenate([jnp.where(low, blocks, theirs), jnp.where(low, theirs, blocks)])
+        bit *= 2
+    return blocks
+
+
+def doubled_up(array, axis, dim):
+    return in_order(doubled(array, axis), dim)
 
 
 def body(right_side, inverse_blocks, coupling, pivots):
@@ -51,9 +72,7 @@
     )
     upper_solved = lax.psum_scatter(first_partial, "pcol", scatter_dimension=0, tiled=True)
     update_partial = jnp.dot(
-        lax.all_gather(upper_solved, "pcol", axis=0, tiled=True),
-        coupling_mat,
-        preferred_element_type=bf16,
+        doubled_up(upper_solved, "pcol", 0), coupling_mat, preferred_element_type=bf16
     )
     update = lax.psum_scatter(update_partial, "prow", scatter_dimension=0, tiled=True)
     lower_ready = (lower_rhs - update.astype(f32)).astype(bf16)

time: 344 us -> 342 us (level)
    all_gather x1 -> x0, waiting for transfers between devices: 31.2 us -> none  [body(): lax.all_gather(upper_solved, 'pcol', axis=0, tiled=True)]
    ppermute x0 -> x2, waiting for transfers between devices: none -> 31 us  [doubled(): theirs = lax.ppermute(blocks, axis, [(i, i ^ bit) for i in range(devices)])]
  transfers between devices with their start and end apart: 7 -> 8, of which waited for: 7 -> 8; matrix products, arithmetic and copies ran while one was open for 11% -> 10% of each run, Pallas kernels for 0% -> 0%
where the time goes in v1:
time: 342 us
  waiting for transfers between devices  223 us (65%)
  local copies, waits for them, and re-layouts  35.9 us (10%)
  matrix products  33.1 us (10%)
  other arithmetic  14.5 us (4%)
  blocking collectives  14 us (4%)
  between operations  13.3 us (4%)
  starting transfers between devices  8.18 us (2%)
    reduce_scatter x1, waiting for transfers between devices, body(): lax.psum_scatter(update_partial, 'prow', scatter_dimension=0, tiled=True)  44.9 us
    all_gather x1, waiting for transfers between devices, body(): lax.all_gather(lower_ready, 'prow', axis=0, tiled=True)  39.6 us
    all_gather x1, waiting for transfers between devices, body(): lax.all_gather(upper_rhs, 'prow', axis=0, tiled=True)  38.3 us
    reduce_scatter x1, waiting for transfers between devices, body(): lax.psum_scatter(first_partial, 'pcol', scatter_dimension=0, tiled=True)  33.9 us
    ppermute x2, waiting for transfers between devices, doubled(): theirs = lax.ppermute(blocks, axis, [(i, i ^ bit) for i in range(devices)])  31 us
    all_to_all x1, waiting for transfers between devices, body(): lax.all_to_all(chosen.reshape(own_cols, rows_axis, share), 'prow', split_...  23.6 us
    dot_general x2, matrix products, solve_with(): lax.dot_general(portion, inverse_mat, contract_last, preferred_element_ty...  18.7 us
    unnamed x12, local copies, waits for them, and re-layouts  15.4 us
  transfers between devices with their start and end apart: 8, of which 8 were waited for; matrix products, arithmetic and copies ran while one was open for 10% of the time, Pallas kernels for 0%

profile of v1, /device:TPU:0, one launch (start us, length us, event | category | flops | bytes accessed | tf_op | source)
XLA Modules:
  0.0 341.9 jit_solution(6951894816708713767)
XLA Ops:
  6.5 4.5 %fusion.9 = bf16[128,2,1024]{2,1,0:T(2,128)(2,1)S(1)} fusion(f32[128,4,1,1024]{3,2,1,0:T(1,128)} %param.4), kind=kLoop, calls=%fused_computation.13 | loop fusion | bytes 1048576 | tf_op jit(solution)/shard_map/slice | solution.py:46
  11.0 0.9 copy.21
  12.0 8.0 %fusion.32 = (bf16[1,1,1,1024,2,1,1024]{6,4,5,3,2,1,0:T(2,128)(2,1)}, bf16[1,1,1,1024,2,1,1024]{6,4,5,3,2,1,0:T(2,128)(2,1)S(1)}) fusion(bf16[2,1,1,1024,2,1,1024]{6,4,5,3,2,1,0:T(2,128)(2,1)} %param.5), kind=kLoop, calls=%fused_computation.78 | loop fusion | bytes 16777216 | tf_op jit(solution)/shard_map/slice | solution.py:80
  20.0 3.4 copy.22
  23.4 38.3 %all-gather.4.cloned.1.call-done = bf16[1024,2048]{1,0:T(8,128)(2,1)} async-done(((bf16[128,2048]{1,0:T(8,128)(2,1)}), bf16[1024,2048]{1,0:T(8,128)(2,1)}) %all-gather.4.cloned.1.call-update) | async-done | bytes 4194320 | tf_op jit(solution)/shard_map/all_gather | solution.py:71
  61.7 9.4 %fusion.33 = bf16[1024,1024]{1,0:T(8,128)(2,1)} fusion(bf16[1024,2048]{1,0:T(8,128)(2,1)} %all-gather.4.cloned.1.call-done, bf16[1024,2048]{1,0:T(8,128)(2,1)} %bitcast.91), kind=kOutput, calls=%fused_computation.79 | convolution fusion | flops 4294967296 | bytes 10485760 | tf_op jit(solution)/shard_map/dot_general | solution.py:68
  71.1 0.2 reduce-scatter.6.cloned.1.call-start
  71.3 33.9 %reduce-scatter.4.cloned.1.call-done = bf16[256,1024]{1,0:T(8,128)(2,1)} async-done(((bf16[1024,1024]{1,0:T(8,128)(2,1)}), bf16[256,1024]{1,0:T(8,128)(2,1)}) %reduce-scatter.4.cloned.1.call-update) | async-done | bytes 524304 | tf_op jit(solution)/shard_map/reduce_scatter | solution.py:73
  105.3 1.5 collective-permute-start
  106.7 12.2 %collective-permute-done = bf16[1,256,1024]{2,1,0:T(8,128)(2,1)S(1)} collective-permute-done((bf16[1,256,1024]{2,1,0:T(8,128)(2,1)}, bf16[1,256,1024]{2,1,0:T(8,128)(2,1)S(1)}, u32[]{:S(2)}, u32[]{:S(2)}) %collective-permute-start) | collective-permute-done | bytes 524320 | tf_op jit(solution)/shard_map/ppermute | solution.py:17
  119.0 1.1 broadcast_select_fusion.3
  120.1 0.1 pad_maximum_fusion.1
  120.2 1.5 collective-permute-start.1
  121.7 3.6 %copy.23 = bf16[128,8,2,1024]{3,1,2,0:T(8,128)(2,1)S(1)} copy(bf16[128,8,2,1024]{3,2,1,0:T(2,128)(2,1)} %bitcast.89) | data formatting | bytes 8388608
  125.4 18.8 %collective-permute-done.1 = bf16[2,256,1024]{2,1,0:T(8,128)(2,1)S(1)} collective-permute-done((bf16[2,256,1024]{2,1,0:T(8,128)(2,1)S(1)}, bf16[2,256,1024]{2,1,0:T(8,128)(2,1)S(1)}, u32[]{:S(2)}, u32[]{:S(2)}) %collective-permute-start.1) | collective-permute-done | bytes 1048608 | tf_op jit(solution)/shard_map/ppermute | solution.py:17
  144.1 0.1 broadcast_select_fusion.1
  144.3 0.2 pad_maximum_fusion
  144.5 6.2 %fusion.34 = bf16[1024,2048]{1,0:T(8,128)(2,1)} fusion(bf16[1024,1024]{1,0:T(8,128)(2,1)S(1)} %bitcast.96, bf16[1024,2048]{1,0:T(8,128)(2,1)S(1)} %bitcast.90), kind=kOutput, calls=%fused_computation.80 | convolution fusion | flops 4294967296 | bytes 10485760 | tf_op jit(solution)/shard_map/dot_general | solution.py:74
  150.7 1.5 copy-done
  152.2 3.2 slice_reduce_fusion
  155.4 0.3 copy.20
  155.8 44.9 %reduce-scatter.6.cloned.1.call-done = bf16[128,2048]{1,0:T(8,128)(2,1)} async-done(((bf16[1024,2048]{1,0:T(8,128)(2,1)}), bf16[128,2048]{1,0:T(8,128)(2,1)}) %reduce-scatter.6.cloned.1.call-update) | async-done | bytes 524304 | tf_op jit(solution)/shard_map/reduce_scatter | solution.py:77
  200.7 1.9 subtract_convert_fusion
  202.7 0.3 reduce-scatter.8.cloned.1.call-start
  203.0 5.6 %copy.24 = bf16[128,8,2,1024]{3,1,2,0:T(8,128)(2,1)} copy(bf16[128,8,2,1024]{3,2,1,0:T(2,128)(2,1)} %bitcast.87) | data formatting | bytes 8388608
  208.6 39.6 %all-gather.6.cloned.1.call-done = bf16[1024,2048]{1,0:T(8,128)(2,1)} async-done(((bf16[128,2048]{1,0:T(8,128)(2,1)}), bf16[1024,2048]{1,0:T(8,128)(2,1)}) %all-gather.6.cloned.1.call-update) | async-done | bytes 4194320 | tf_op jit(solution)/shard_map/all_gather | solution.py:80
  248.2 9.4 %fusion.35 = bf16[1024,1024]{1,0:T(8,128)(2,1)} fusion(bf16[1024,2048]{1,0:T(8,128)(2,1)} %all-gather.6.cloned.1.call-done, bf16[1024,2048]{1,0:T(8,128)(2,1)} %bitcast.92), kind=kOutput, calls=%fused_computation.81 | convolution fusion | flops 4294967296 | bytes 10485760 | tf_op jit(solution)/shard_map/dot_general | solution.py:68
  257.6 14.0 %all-gather = s32[8,1,2048]{2,1,0:T(1,128)S(1)} all-gather(s32[1,1,2048]{2,1,0:T(1,128)S(1)} %bitcast.100), channel_id=1, replica_groups=mesh['prow'=8,'pcol'=4] {'prow'}, dimensions={0}, use_global_device_ids=true | all-gather | bytes 73728 | tf_op jit(solution)/shard_map/all_gather | solution.py:50
  271.6 0.1 convert_bitcast_fusion
  271.7 2.3 reduce-window.14
  274.0 0.3 slice_reduce_fusion.2
  274.3 0.2 reduce-window.15
  274.5 0.1 add_bitcast_fusion
  274.6 0.1 fusion.17
  274.6 5.7 %select_reduce_fusion = s32[8,256]{1,0:T(8,128)S(1)} fusion(s32[8,2048]{1,0:T(8,128)S(1)} %get-tuple-element.13, s32[8,2048]{1,0:T(8,128)S(1)} %get-tuple-element.14), kind=kLoop, calls=%fused_computation.2 | loop fusion | flops 12580864 | bytes 139264 | tf_op jit(solution)/shard_map/reduce_sum | solution.py:61
  280.4 11.3 %reduce-scatter.8.cloned.1.call-done = bf16[256,1024]{1,0:T(8,128)(2,1)} async-done(((bf16[1024,1024]{1,0:T(8,128)(2,1)}), bf16[256,1024]{1,0:T(8,128)(2,1)}) %reduce-scatter.8.cloned.1.call-update) | async-done | bytes 524304 | tf_op jit(solution)/shard_map/reduce_scatter | solution.py:82
  291.7 4.4 %fusion.3 = bf16[256,2048]{1,0:T(8,128)(2,1)S(1)} fusion(s32[2048]{0:T(1024)S(1)} %bitcast.105, bf16[256,1024]{1,0:T(8,128)(2,1)S(1)} %copy-done.1, bf16[256,1024]{1,0:T(8,128)(2,1)} %reduce-scatter.8.cloned.1.call-done), kind=kOutput, calls=%fused_computation.6 | convolution fusion | flops 2153775104 | bytes 2105344 | tf_op jit(solution)/shard_map/dot_general | solution.py:87
  296.1 1.0 copy.38
  297.2 4.6 %all-to-all-start = ((bf16[256,8,256]{2,0,1:T(8,128)(2,1)}), bf16[256,8,256]{2,0,1:T(8,128)(2,1)S(1)}, u32[]{:S(2)}, u32[]{:S(2)}) async-start(bf16[256,8,256]{2,0,1:T(8,128)(2,1)} %bitcast.84), calls=%async_computation.3 | async-start | bytes 2097152 | tf_op jit(solution)/shard_map/all_to_all | solution.py:88
  301.8 2.3 reduce-window.16
  304.1 0.3 slice_reduce_fusion.1
  304.4 0.2 reduce-window.19
  304.6 0.1 select_reduce_fusion.1
  304.7 23.6 %all-to-all-done = bf16[256,8,256]{2,0,1:T(8,128)(2,1)S(1)} async-done(((bf16[256,8,256]{2,0,1:T(8,128)(2,1)}), bf16[256,8,256]{2,0,1:T(8,128)(2,1)S(1)}, u32[]{:S(2)}, u32[]{:S(2)}) %all-to-all-start) | async-done | bytes 1048608 | tf_op jit(solution)/shard_map/all_to_all | solution.py:88
  328.4 0.6 copy.15
  329.0 0.5 reshape.157
  329.5 3.8 %fusion.6 = bf16[256,2,1,1024]{3,0,1,2:T(8,128)(2,1)S(1)} fusion(bf16[256,2048,1]{1,0,2:T(8,128)(2,1)S(1)} %reshape.157, s32[2,1024]{1,0:T(2,128)S(1)} %fusion.27), kind=kOutput, calls=%fused_computation.10 | convolution fusion | flops 2151677952 | bytes 2105344 | tf_op jit(solution)/shard_map/dot_general | solution.py:92
  333.3 2.0 copy.16
  (19 shorter events, 0.3 us)
Async XLA Ops:
  6.5 55.2 %all-gather.4.cloned.1.call-start = ((), (), s32[]{:S(2)}) async-start(), calls=%async_computation.4 | async-start | bytes 4718592 | tf_op jit(solution)/shard_map/all_gather | solution.py:71
  12.0 93.3 %reduce-scatter.4.cloned.1.call-start = ((), (), s32[]{:S(2)}) async-start(), calls=%async_computation.5 | async-start | bytes 2621440 | tf_op jit(solution)/shard_map/reduce_scatter | solution.py:73
  71.1 129.6 %reduce-scatter.6.cloned.1.call-start = ((), (), s32[]{:S(2)}) async-start(), calls=%async_computation.6 | async-start | bytes 4718592 | tf_op jit(solution)/shard_map/reduce_scatter | solution.py:77
  105.3 13.7 %collective-permute-start = (bf16[1,256,1024]{2,1,0:T(8,128)(2,1)}, bf16[1,256,1024]{2,1,0:T(8,128)(2,1)S(1)}, u32[]{:S(2)}, u32[]{:S(2)}) collective-permute-start(bf16[1,256,1024]{2,1,0:T(8,128)(2,1)} %bitcast.99), channel_id=1, source_target_pairs={{0,1},{1,0},{2,3},{3,2},{4,5},{5,4},{6,7},{7,6},{8,9},{9,8},{10,11... | collective-permute-start | bytes 1572872 | tf_op jit(solution)/shard_map/ppermute | solution.py:17
  120.2 23.9 %collective-permute-start.1 = (bf16[2,256,1024]{2,1,0:T(8,128)(2,1)S(1)}, bf16[2,256,1024]{2,1,0:T(8,128)(2,1)S(1)}, u32[]{:S(2)}, u32[]{:S(2)}) collective-permute-start(bf16[2,256,1024]{2,1,0:T(8,128)(2,1)S(1)} %pad_maximum_fusion.1), channel_id=1, source_target_pairs={{0,2},{1,3},{2,0},{3,1},{4,6},{5,7},{6,4},{7,5},{8,10},{9,11},{10,... | collective-permute-start | bytes 3145736 | tf_op jit(solution)/shard_map/ppermute | solution.py:17
  150.6 1.6 copy-start
  150.7 97.5 %all-gather.6.cloned.1.call-start = ((), (), s32[]{:S(2)}) async-start(), calls=%async_computation.7 | async-start | bytes 4718592 | tf_op jit(solution)/shard_map/all_gather | solution.py:80
  202.7 89.0 %reduce-scatter.8.cloned.1.call-start = ((), (), s32[]{:S(2)}) async-start(), calls=%async_computation.8 | async-start | bytes 2621440 | tf_op jit(solution)/shard_map/reduce_scatter | solution.py:82
  248.2 9.4 %copy-start.2 = (s32[2,1,1024]{2,1,0:T(1,128)S(1)}, s32[2,1,1024]{2,1,0:T(1,128)}, u32[]{:S(2)}) copy-start(s32[2,1,1024]{2,1,0:T(1,128)} %param.7) | copy-start | bytes 24580
  248.2 43.5 %copy-start.1 = (bf16[256,1024]{1,0:T(8,128)(2,1)S(1)}, bf16[256,1024]{1,0:T(8,128)(2,1)}, u32[]{:S(2)}) copy-start(bf16[256,1024]{1,0:T(8,128)(2,1)} %reduce-scatter.4.cloned.1.call-done) | copy-start | bytes 1572868
  297.2 31.2 %all-to-all-start = ((bf16[256,8,256]{2,0,1:T(8,128)(2,1)}), bf16[256,8,256]{2,0,1:T(8,128)(2,1)S(1)}, u32[]{:S(2)}, u32[]{:S(2)}) async-start(bf16[256,8,256]{2,0,1:T(8,128)(2,1)} %bitcast.84), calls=%async_computation.3 | async-start | bytes 2097152 | tf_op jit(solution)/shard_map/all_to_all | solution.py:88
Sparse Core Ops, SparseCore 0:
  12.1 49.5 all-gather.3
  71.2 33.9 reduce-scatter.3
  150.8 49.8 reduce-scatter.5
  202.8 45.3 all-gather.5
  257.7 33.9 reduce-scatter.7
